TPU v7x, 32 devices: a whole 2x2x4 slice. The times are simulated.
32 devices in a mesh: row: 8 (over z, x), col: 4 (over y, core).
Axes of the slice: x: 2, y: 2, z: 4, core: 2. Of those that a mesh axis runs over, the one named last changes fastest.
Arguments:
- solution_field: float32 [32, 32768], P(None, ('row', 'col')), may hold values from -6 to 6
- residual: float32 [32, 32768], P(None, ('row', 'col')), may hold values from -420 to 420
- direction: float32 [32, 32768], P(None, ('row', 'col')), may hold values from -420 to 420
- positions: bfloat16 [2, 32768], P(None, ('row', 'col')), may hold values from -6 to 6
- tile_pairs: int32 [2, 49152], P(None, ('row', 'col')), may hold values from 0 to 63, as said below
- pair_count: int32 [32], P(('row', 'col')), may hold values from 0 to 1536, as said below
Outputs:
- solution_next: float32 [32, 32768], P(None, ('row', 'col'))
- residual_next: float32 [32, 32768], P(None, ('row', 'col'))
- direction_next: float32 [32, 32768], P(None, ('row', 'col'))
Inputs may be any that keep to these rules, and one draw needn't show every extreme that they name: `tile_pairs`: row 0 holds local row tiles below 32, row 1 local column tiles below 64. The live pairs of one slot block are distinct and strictly upper (I < J); entries in slots that are not live are in range but carry nothing. `pair_count`: some slot block is full in every draw.
All inputs are finite; a program needn't handle non-finite values.
Results may differ from a plain program's by a relative error of at most 0.007.
Values may be sent and summed in bfloat16 or wider, within the bound.
A program may use at most 64 MiB of HBM per device.

v0:
```python
import functools
import math

import jax
import jax.numpy as jnp
from jax import lax
from jax.experimental import pallas as pl
from jax.experimental.pallas import tpu as pltpu
from jax.sharding import PartitionSpec as P

TILE = 128
FEATURES = 16
UNROLL = 8
BLOCK = 2 * TILE

AMPLITUDE = 0.025
NUGGET = 2.0
RADIUS = 1.0
HIGHEST = lax.Precision.HIGHEST


def cross_gram_matrix(former, latter):
    return lax.dot_general(
        former,
        latter,
        (((1,), (1,)), ((), ())),
        precision=HIGHEST,
        preferred_element_type=jnp.float32,
    )


def apply_left(matrix, vectors):
    return jnp.dot(matrix.T, vectors, precision=HIGHEST)


def symmetric_solve(matrix, target):
    balanced = 0.5 * (matrix + matrix.T)
    factor = jnp.linalg.cholesky(balanced)
    middle = lax.linalg.triangular_solve(factor, target, left_side=True, lower=True)
    return lax.linalg.triangular_solve(factor, middle, left_side=True, lower=True, transpose_a=True)


def split_three(value):
    high = lax.reduce_precision(value, 8, 7)
    rest = value - high
    middle = lax.reduce_precision(rest, 8, 7)
    return high, middle, rest - middle


def features(positions):
    coord = positions.astype(jnp.float32)
    x, y = coord[0], coord[1]
    high, middle, low = split_three(x * x + y * y)
    one = jnp.ones_like(x)
    zero = jnp.zeros_like(x)
    pad = [zero] * (FEATURES - 8)
    near = jnp.stack([x, y, high, middle, low, one, one, one] + pad)
    far = 16.0 * jnp.stack([-2.0 * x, -2.0 * y, one, one, one, high, middle, low] + pad)
    return near.astype(jnp.bfloat16), far.astype(jnp.bfloat16)


def kernel_of(square, floor):
    square = jnp.minimum(jnp.maximum(square, floor), 16.0)
    quad = square * lax.rsqrt(square)
    remain = 4.0 - quad
    remain = remain * remain
    return (remain * remain * (quad + 1.0)).astype(jnp.bfloat16)


def block_of(near, far, floors):
    square = jnp.dot(near, far, preferred_element_type=jnp.float32)
    rows = []
    for a in range(2):
        part = square[a * TILE : (a + 1) * TILE]
        row = [kernel_of(part[:, b * TILE : (b + 1) * TILE], floors[a][b]) for b in range(2)]
        rows.append(jnp.concatenate(row, axis=1))
    return jnp.concatenate(rows, axis=0)


def times_transposed(vectors, block):
    return lax.dot_general(
        vectors, block, (((1,), (1,)), ((), ())), preferred_element_type=jnp.float32
    )


def pair_kernel(
    cells, count, near, row_pack, col_pack, row_out, col_out, own_out, col_acc, floor
):
    row_blocks, col_blocks = row_pack.shape[0], col_pack.shape[0]
    probes = row_out.shape[1]
    row_vec, col_vec = row_pack.at[:, :probes], col_pack.at[:, :probes]
    far = col_pack.at[:, probes:]
    own_blocks = own_out.shape[0]
    stride = 2 * col_blocks
    scale = AMPLITUDE / 256.0
    live = count[0]
    unroll = math.gcd(UNROLL, col_blocks)
    col_acc[...] = jnp.zeros_like(col_acc)

    @pl.loop(0, 2 * row_blocks * stride // 16)
    def _(step):
        for k in range(16):
            floor[step * 16 + k] = 16.0

    def mark(slot):
        floor[cells[slot]] = 1e-20

    whole = live // 8

    @pl.loop(0, whole)
    def _(step):
        for k in range(8):
            mark(step * 8 + k)

    @pl.loop(whole * 8, live)
    def _(slot):
        mark(slot)

    def products(i, j):
        base = 2 * i * stride + 2 * j
        floors = [[floor[base + a * stride + b] for b in range(2)] for a in range(2)]
        block = block_of(near[i], far[j], floors)
        forward = times_transposed(col_vec[j], block)
        backward = jnp.dot(row_vec[i], block, preferred_element_type=jnp.float32)
        return forward, backward

    @pl.loop(0, row_blocks)
    def _(i):
        def several(step, total):
            results = [products(i, step * unroll + k) for k in range(unroll)]
            for k, (forward, backward) in enumerate(results):
                total = total + forward
                col_acc[step * unroll + k] += backward
            return total

        start = jnp.zeros(row_out.shape[1:], jnp.float32)
        total = lax.fori_loop(0, col_blocks // unroll, several, start)
        row_out[i] = (scale * total).astype(row_out.dtype)

    row_base = lax.axis_index("col") * own_blocks
    col_base = lax.axis_index("row") * own_blocks

    @pl.loop(0, own_blocks)
    def _(t):
        block = block_of(near[row_base + t], far[col_base + t], [[1e-20, 16.0], [16.0, 1e-20]])
        own_out[t] = scale * times_transposed(col_vec[col_base + t], block)

    col_out[...] = (scale * col_acc[...]).astype(col_out.dtype)


MESH = pl.DeviceIdType.MESH


def greet(sizes):
    barrier = pltpu.get_barrier_semaphore()
    for axis, size in sizes:
        me = lax.axis_index(axis)
        for k in range(1, size):
            peer = lax.rem(me + k, size)
            pl.semaphore_signal(barrier, inc=1, device_id={axis: peer}, device_id_type=MESH)
    pl.semaphore_wait(barrier, sum(size - 1 for _, size in sizes))


class Exchange:
    def __init__(self, axis, size, source, landing, send_sem, recv_sem):
        self.axis, self.size, self.source, self.landing = axis, size, source, landing
        self.send_sem, self.recv_sem = send_sem, recv_sem
        self.me = lax.axis_index(axis)

    def copy(self, k, source, slot, peer):
        return pltpu.make_async_remote_copy(
            src_ref=source,
            dst_ref=self.landing.at[slot],
            send_sem=self.send_sem.at[k],
            recv_sem=self.recv_sem.at[k],
            device_id={self.axis: peer},
            device_id_type=MESH,
        )

    def outgoing(self, k):
        peer = lax.rem(self.me + k, self.size)
        return self.copy(k, self.source(peer), self.me, peer)

    def start(self):
        for k in range(1, self.size):
            self.outgoing(k).start()

    def wait_recv(self):
        for k in range(1, self.size):
            origin = lax.rem(self.me + self.size - k, self.size)
            self.copy(k, self.landing.at[origin], origin, origin).wait_recv()

    def wait_send(self):
        for k in range(1, self.size):
            self.outgoing(k).wait_send()


def gather_kernel(
    n_row, n_col, row_in, col_in, row_out, col_out, own_sem, row_send, row_recv, col_send, col_recv
):
    row_me, col_me = lax.axis_index("col"), lax.axis_index("row")
    own = [
        pltpu.make_async_copy(row_in, row_out.at[row_me], own_sem.at[0]),
        pltpu.make_async_copy(col_in, col_out.at[col_me], own_sem.at[1]),
    ]
    for copy in own:
        copy.start()
    greet((("row", n_row), ("col", n_col)))
    over_row = Exchange("row", n_row, lambda peer: col_in, col_out, col_send, col_recv)
    over_col = Exchange("col", n_col, lambda peer: row_in, row_out, row_send, row_recv)
    over_row.start()
    over_col.start()
    for copy in own:
        copy.wait()
    for exchange in (over_col, over_row):
        exchange.wait_recv()
        exchange.wait_send()


def image_kernel(
    n_row,
    n_col,
    row_part,
    col_part,
    own_product,
    direction,
    residual,
    applied,
    gram,
    row_land,
    col_land,
    gram_own,
    gram_half,
    gram_col,
    gram_row,
    *sems,
):
    blocks = own_product.shape[0]
    row_me, col_me = lax.axis_index("col"), lax.axis_index("row")
    greet((("row", n_row), ("col", n_col)))

    def part_of(parts):
        return lambda peer: parts.at[pl.ds(peer * blocks, blocks)]

    over_row = Exchange("row", n_row, part_of(col_part), col_land, sems[0], sems[1])
    over_col = Exchange("col", n_col, part_of(row_part), row_land, sems[2], sems[3])
    over_row.start()
    over_col.start()
    total = own_product[...]
    total += row_part[pl.ds(row_me * blocks, blocks)].astype(jnp.float32)
    total += col_part[pl.ds(col_me * blocks, blocks)].astype(jnp.float32)
    over_col.wait_recv()
    for k in range(1, n_col):
        total += row_land[lax.rem(row_me + k, n_col)].astype(jnp.float32)
    over_row.wait_recv()
    for k in range(1, n_row):
        total += col_land[lax.rem(col_me + k, n_row)].astype(jnp.float32)
    flat = jnp.concatenate([total[b] for b in range(blocks)], axis=1)
    image = NUGGET * direction[...] + flat
    applied[...] = image
    left = jnp.concatenate([image, residual[...]], axis=0)
    right = jnp.concatenate([left, direction[...]], axis=0)
    product = cross_gram_matrix(left, right)
    lanes = gram_own.shape[1] - product.shape[1]
    gram_own[...] = jnp.concatenate(
        [product, jnp.zeros((product.shape[0], lanes), jnp.float32)], axis=1
    )
    gram_over_col = Exchange("col", n_col, lambda peer: gram_own, gram_col, sems[4], sems[5])
    gram_over_col.start()
    gram_over_col.wait_recv()
    half = gram_own[...]
    for k in range(1, n_col):
        half += gram_col[lax.rem(row_me + k, n_col)]
    gram_half[...] = half
    gram_over_row = Exchange("row", n_row, lambda peer: gram_half, gram_row, sems[6], sems[7])
    gram_over_row.start()
    gram_over_row.wait_recv()
    whole = gram_half[...]
    for k in range(1, n_row):
        whole += gram_row[lax.rem(col_me + k, n_row)]
    gram[...] = whole
    for exchange in (over_row, over_col, gram_over_col, gram_over_row):
        exchange.wait_send()


def block_major(array):
    rows, points = array.shape
    return array.reshape(rows, points // BLOCK, BLOCK).transpose(1, 0, 2)


def on_device(solution_field, residual, direction, positions, tile_pairs, pair_count):
    probes, own_points = direction.shape
    own_blocks = own_points // BLOCK
    own_vec = block_major(direction.astype(jnp.bfloat16))
    near, far = features(positions)
    n_row, n_col = lax.axis_size("row"), lax.axis_size("col")
    vmem = pl.BlockSpec(memory_space=pltpu.VMEM)
    smem = pl.BlockSpec(memory_space=pltpu.SMEM)
    hbm = pl.BlockSpec(memory_space=pl.ANY)
    row_sem, col_sem = pltpu.SemaphoreType.DMA((n_col,)), pltpu.SemaphoreType.DMA((n_row,))
    row_in = jnp.concatenate([own_vec, block_major(near)], axis=1)
    col_in = jnp.concatenate([own_vec, block_major(far)], axis=1)
    row_pack, col_pack = pl.pallas_call(
        functools.partial(gather_kernel, n_row, n_col),
        out_shape=(
            jax.ShapeDtypeStruct((n_col, *row_in.shape), jnp.bfloat16),
            jax.ShapeDtypeStruct((n_row, *col_in.shape), jnp.bfloat16),
        ),
        in_specs=[vmem, vmem],
        out_specs=(hbm, hbm),
        scratch_shapes=[pltpu.SemaphoreType.DMA((2,)), row_sem, row_sem, col_sem, col_sem],
        compiler_params=pltpu.CompilerParams(collective_id=0, has_side_effects=True),
        name="gather",
    )(row_in, col_in)
    row_pack = row_pack.reshape(-1, *row_in.shape[1:])
    col_pack = col_pack.reshape(-1, *col_in.shape[1:])
    near = row_pack[:, probes:].transpose(0, 2, 1)
    row_blocks, col_blocks = row_pack.shape[0], col_pack.shape[0]
    cells = tile_pairs[0] * (2 * col_blocks) + tile_pairs[1]
    row_part, col_part, own_product = pl.pallas_call(
        pair_kernel,
        out_shape=(
            jax.ShapeDtypeStruct((row_blocks, probes, BLOCK), jnp.bfloat16),
            jax.ShapeDtypeStruct((col_blocks, probes, BLOCK), jnp.bfloat16),
            jax.ShapeDtypeStruct((own_blocks, probes, BLOCK), jnp.float32),
        ),
        in_specs=[smem, smem, vmem, vmem, vmem],
        out_specs=(vmem, vmem, vmem),
        scratch_shapes=[
            pltpu.VMEM((col_blocks, probes, BLOCK), jnp.float32),
            pltpu.SMEM((4 * row_blocks * col_blocks,), jnp.float32),
        ],
        name="pairs",
    )(cells, pair_count, near, row_pack, col_pack)
    applied, gram = pl.pallas_call(
        functools.partial(image_kernel, n_row, n_col),
        out_shape=(
            jax.ShapeDtypeStruct((probes, own_points), jnp.float32),
            jax.ShapeDtypeStruct((2 * probes, TILE), jnp.float32),
        ),
        in_specs=[vmem] * 5,
        out_specs=(vmem, vmem),
        scratch_shapes=[
            pltpu.VMEM((n_col, *own_product.shape), jnp.bfloat16),
            pltpu.VMEM((n_row, *own_product.shape), jnp.bfloat16),
            pltpu.VMEM((2 * probes, TILE), jnp.float32),
            pltpu.VMEM((2 * probes, TILE), jnp.float32),
            pltpu.VMEM((n_col, 2 * probes, TILE), jnp.float32),
            pltpu.VMEM((n_row, 2 * probes, TILE), jnp.float32),
            col_sem,
            col_sem,
            row_sem,
            row_sem,
            row_sem,
            row_sem,
            col_sem,
            col_sem,
        ],
        compiler_params=pltpu.CompilerParams(collective_id=1, has_side_effects=True),
        name="image",
    )(row_part, col_part, own_product, direction, residual)
    square, image_resid = gram[:probes, :probes], gram[:probes, probes : 2 * probes]
    norm_old = gram[probes:, probes : 2 * probes]
    curvature = gram[:probes, 2 * probes : 3 * probes].T
    crossing = gram[probes:, 2 * probes : 3 * probes].T
    step_size = symmetric_solve(curvature, crossing)
    residual_next = residual - apply_left(step_size, applied)
    shifted = jnp.dot(step_size.T, image_resid, precision=HIGHEST)
    quadratic = jnp.dot(
        step_size.T, jnp.dot(square, step_size, precision=HIGHEST), precision=HIGHEST
    )
    norm_new = norm_old - shifted - shifted.T + quadratic
    solution_next = solution_field + apply_left(step_size, direction)
    mix_weight = symmetric_solve(norm_old, norm_new)
    direction_next = residual_next + apply_left(mix_weight, direction)
    return (solution_next, residual_next, direction_next)


def solution(mesh):
    whole = P(None, ("row", "col"))
    return jax.shard_map(
        on_device,
        mesh=mesh,
        in_specs=(whole, whole, whole, whole, whole, P(("row", "col"))),
        out_specs=(whole, whole, whole),
        check_vma=False,
    )
```

profile of v0, /device:TPU:0, one launch (start us, length us, event | category | flops | bytes accessed | tf_op | source)
XLA Modules:
  0.0 195.3 jit_solution(7271408617441229180)
XLA Ops:
  1.3 0.0 copy-start.7
  1.3 1.4 add_reduce_fusion.cells
  2.7 0.0 copy-done.7
  2.8 0.1 stack.46
  2.9 0.0 copy-start
  2.9 0.1 stack.52
  3.0 0.8 copy-done
  3.8 0.7 pad_maximum_fusion
  4.5 20.0 %gather.1 = (bf16[4,4,48,256]{3,2,1,0:T(8,128)(2,1)}, bf16[8,4,48,256]{3,2,1,0:T(8,128)(2,1)}) custom-call(bf16[4,48,256]{2,1,0:T(8,128)(2,1)} %get-tuple-element.23.row_in, bf16[4,48,256]{2,1,0:T(8,128)(2,1)} %get-tuple-element.22.col_in), custom_call_target="tpu_custom_call" | custom-call | tf_op jit(solution)/shard_map/gather/pallas_call | solution.py:303
  24.5 0.9 slice_bitcast_fusion
  25.5 1.3 copy.17.near
  26.8 120.2 %pairs.1 = (bf16[16,32,256]{2,1,0:T(8,128)(2,1)}, bf16[32,32,256]{2,1,0:T(8,128)(2,1)}, f32[4,32,256]{2,1,0:T(8,128)}) custom-call(s32[1536]{0:T(1024)} %add_reduce_fusion.cells, s32[1]{0:T(128)S(6)} %copy.27.count, bf16[16,256,16]{2,1,0:T(8,128)(2,1)} %copy.17.near, bf16[16,48,256]{2,1,0:T(8,128)(2,1)} %bitcast.74, bf16[32,48,256]{2,1,0:T(8,128)(2,1)} %bitcast.72), custom_call_target="tpu_custom_call" | custom-call | tf_op jit(solution)/shard_map/pairs/pallas_call | solution.py:320
  147.0 29.6 %image.1 = (f32[32,1024]{1,0:T(8,128)}, f32[64,128]{1,0:T(8,128)}) custom-call(bf16[16,32,256]{2,1,0:T(8,128)(2,1)} %get-tuple-element.15.row_part, bf16[32,32,256]{2,1,0:T(8,128)(2,1)} %get-tuple-element.16.col_part, f32[4,32,256]{2,1,0:T(8,128)} %get-tuple-element.17.own_product, f32[32,1024]{1,0:T(8,128)} %direction.1, f32[32,1024]{1,0:T(8,128)} %residual.1), custom_call_target="tpu_custom_call" | custom-call | tf_op jit(solution)/shard_map/image/pallas_call | solution.py:335
  176.6 0.0 copy-start.4
  176.6 0.9 slice.46
  177.4 0.1 copy.21
  177.5 0.0 copy-done.4
  177.5 0.1 fusion.8
  177.6 0.1 copy.22
  177.7 2.9 %cholesky.55 = f32[32,32]{1,0:T(8,128)S(1)} custom-call(f32[32,32]{1,0:T(8,128)S(1)} %fusion.7), custom_call_target="Cholesky" | custom-call | tf_op jit(solution)/shard_map/jit(cholesky)/cholesky | solution.py:38
  180.6 0.6 compare_reduce_fusion
  181.3 0.7 fusion.2
  181.9 2.4 %custom-call.13 = f32[1,32,32]{1,2,0:T(8,128)S(1)} custom-call(f32[1,32,32]{2,1,0:T(8,128)S(1)} %fusion.2), custom_call_target="InvertDiagBlocksLowerTriangular" | custom-call | tf_op jit(solution)/shard_map/triangular_solve/custom-call.2 | solution.py:40
  184.4 0.1 copy.18
  184.5 0.1 copy.19
  184.6 0.0 copy-start.2
  184.6 0.1 copy.20
  184.7 2.9 %cholesky.44 = f32[32,32]{1,0:T(8,128)S(1)} custom-call(f32[32,32]{1,0:T(8,128)S(1)} %fusion.14), custom_call_target="Cholesky" | custom-call | tf_op jit(solution)/shard_map/jit(cholesky)/cholesky | solution.py:38
  187.6 0.6 compare_reduce_fusion.1
  188.3 0.7 fusion.1
  188.9 2.4 %custom-call.11 = f32[1,32,32]{1,2,0:T(8,128)S(1)} custom-call(f32[1,32,32]{2,1,0:T(8,128)S(1)} %fusion.1), custom_call_target="InvertDiagBlocksLowerTriangular" | custom-call | tf_op jit(solution)/shard_map/triangular_solve/custom-call.2 | solution.py:40
  191.4 0.3 fusion.9
  191.6 0.1 fusion.12
  191.8 0.0 copy-done.2
  191.8 0.0 copy-done.6
  191.8 0.3 convolution_subtract_fusion
  192.1 0.0 copy-start.3
  192.1 0.2 fusion.17
  192.4 0.1 copy.23
  192.5 0.1 fusion.15
  192.6 0.2 convolution_add_fusion.2
  192.8 0.2 fusion.3
  193.0 0.1 fusion.5
  193.2 0.0 copy-done.3
  193.2 0.2 copy-done.1
  193.4 1.0 convolution_add_fusion
  194.3 0.0 copy-done.5
  194.3 1.0 convolution_add_fusion.1
  (24 shorter events, 0.2 us)
Async XLA Ops:
  1.3 1.4 copy-start.7
  2.9 0.9 copy-start
  176.6 0.9 copy-start.4
  184.6 7.2 %copy-start.2 = (f32[32,1024]{1,0:T(8,128)S(1)}, f32[32,1024]{1,0:T(8,128)}, u32[]{:S(2)}) copy-start(f32[32,1024]{1,0:T(8,128)} %residual.1) | copy-start | bytes 393220
  184.6 7.2 %copy-start.6 = (f32[32,1024]{1,0:T(8,128)S(1)}, f32[32,1024]{1,0:T(8,128)}, u32[]{:S(2)}) copy-start(f32[32,1024]{1,0:T(8,128)} %get-tuple-element.19) | copy-start | bytes 393220
  192.1 1.1 copy-start.3
  192.5 0.9 copy-start.1
  193.4 1.0 copy-start.5
where the time goes:
time: 196 us; the launch traced here: 195 us
  Pallas kernels  170 us (87%)
  other arithmetic  15.6 us (8%)
  local copies, waits for them, and re-layouts  4.76 us (2%)
  matrix products  3.59 us (2%)
    pallas_call x1, Pallas kernels, on_device(): pl.pallas_call(pair_kernel, out_shape=(jax.ShapeDtypeStruct((row_blocks,...  120 us
    pallas_call x1, Pallas kernels, on_device(): pl.pallas_call(functools.partial(image_kernel, n_row, n_col), out_shape=(...  29.6 us
    pallas_call x1, Pallas kernels, on_device(): pl.pallas_call(functools.partial(gather_kernel, n_row, n_col), out_shape=...  20 us
    another operation x6, other arithmetic, symmetric_solve(): factor = jnp.linalg.cholesky(balanced)  7.2 us
    another operation x4, other arithmetic, symmetric_solve(): lax.linalg.triangular_solve(factor, middle, left_side=True, lower=True, t...  6.17 us

commit v1 on v0

v1 whole, which is shorter than its diff:
```python
import functools
import itertools

import jax
import jax.numpy as jnp
from jax import lax
from jax.experimental import pallas as pl
from jax.experimental.pallas import tpu as pltpu
from jax.sharding import PartitionSpec as P

TILE = 128
BLOCK = 2 * TILE

AMPLITUDE = 0.025
NUGGET = 2.0
SCALE = 4.0
FAR_AWAY = 128.0
HIGHEST = lax.Precision.HIGHEST
MESH = pl.DeviceIdType.MESH
F32 = jnp.float32
BF16 = jnp.bfloat16


def cross_gram_matrix(former, latter):
    return lax.dot_general(
        former, latter, (((1,), (1,)), ((), ())), precision=HIGHEST, preferred_element_type=F32
    )


def apply_left(matrix, vectors):
    return jnp.dot(matrix.T, vectors, precision=HIGHEST)


def symmetric_solve(matrix, target):
    balanced = 0.5 * (matrix + matrix.T)
    factor = jnp.linalg.cholesky(balanced)
    middle = lax.linalg.triangular_solve(factor, target, left_side=True, lower=True)
    return lax.linalg.triangular_solve(factor, middle, left_side=True, lower=True, transpose_a=True)


@functools.lru_cache(None)
def cover_of(n_row, n_col):
    every = [(r, c) for r in range(n_row) for c in range(n_col)]

    def minus(a, b):
        return ((a[0] - b[0]) % n_row, (a[1] - b[1]) % n_col)

    def cost(e):
        return min(e[0], n_row - e[0]) + min(e[1], n_col - e[1])

    order = sorted(every[1:], key=lambda e: (cost(e), e))
    total = len(every) - 1
    budget = [20000]

    def extend(chosen, seen, start, size):
        if len(chosen) == size:
            return chosen if len(seen) == total else None
        budget[0] -= 1
        rest = size - len(chosen)
        most = sum(2 * (len(chosen) + k) for k in range(rest))
        if budget[0] < 0 or len(seen) + most < total:
            return None
        for k in range(start, len(order)):
            e = order[k]
            new = {minus(e, x) for x in chosen} | {minus(x, e) for x in chosen}
            found = extend(chosen + [e], seen | new, k + 1, size)
            if found:
                return found
        return None

    size = 1
    while size * (size - 1) < total:
        size += 1
    for k in (size, size + 1):
        budget[0] = 20000
        found = extend([(0, 0)], set(), 0, k)
        if found:
            return tuple(found)
    chosen, seen = [(0, 0)], set()
    while len(seen) < total:
        gains = []
        for e in order:
            new = {minus(e, x) for x in chosen} | {minus(x, e) for x in chosen}
            gains.append((-len((new | seen) - {(0, 0)}), cost(e), e))
        e = min(gains)[2]
        seen |= {minus(e, x) for x in chosen} | {minus(x, e) for x in chosen}
        seen.discard((0, 0))
        chosen.append(e)
    return tuple(chosen)


@functools.lru_cache(None)
def units_of(n_row, n_col):
    cover = cover_of(n_row, n_col)
    found = {}
    for i, j in itertools.permutations(range(len(cover)), 2):
        delta = ((cover[j][0] - cover[i][0]) % n_row, (cover[j][1] - cover[i][1]) % n_col)
        found.setdefault(delta, (i, j))
    return tuple(sorted(found.values(), key=lambda u: (max(u), min(u), u)))


def holders_of(n_row, n_col):
    cover = cover_of(n_row, n_col)
    return sorted({(a[0], b[1]) for a in cover for b in cover} - {(0, 0)})


def group_of(n_row, n_col, tiles):
    group = max(1, TILE // (n_row * tiles))
    while n_col % group:
        group -= 1
    return group


def log2(value):
    assert value & (value - 1) == 0
    return value.bit_length() - 1


def pick(index, values):
    result = jnp.int32(values[0])
    for k, value in enumerate(values[1:], 1):
        result = jnp.where(index == k, jnp.int32(value), result)
    return result


class Ring:
    def __init__(self, n_row, n_col):
        self.n_row, self.n_col = n_row, n_col
        self.row, self.col = lax.axis_index("row"), lax.axis_index("col")

    def plus(self, offset):
        return lax.rem(self.row + offset[0], self.n_row), lax.rem(self.col + offset[1], self.n_col)

    def minus(self, offset):
        return self.plus((self.n_row - offset[0], self.n_col - offset[1]))

    def flat(self, place):
        return place[0] * self.n_col + place[1]

    def greet(self):
        barrier = pltpu.get_barrier_semaphore()
        offsets = [(r, c) for r in range(self.n_row) for c in range(self.n_col)][1:]
        for offset in offsets:
            row, col = self.plus(offset)
            pl.semaphore_signal(
                barrier, inc=1, device_id={"row": row, "col": col}, device_id_type=MESH
            )
        pl.semaphore_wait(barrier, len(offsets))


def remote(source, landing, send_sem, recv_sem, place):
    return pltpu.make_async_remote_copy(
        src_ref=source,
        dst_ref=landing,
        send_sem=send_sem,
        recv_sem=recv_sem,
        device_id={"row": place[0], "col": place[1]},
        device_id_type=MESH,
    )


def one_hot(size, index, live=None):
    slots = index.shape[1]
    hit = lax.broadcasted_iota(jnp.int32, (size, slots), 0) == index
    if live is not None:
        hit = hit & live
    return jnp.where(hit, 1.0, 0.0).astype(BF16)


def pattern(ring, tiles, group, tile_pairs, count):
    rows, cols = tile_pairs[0:1, :], tile_pairs[1:2, :]
    live = lax.broadcasted_iota(jnp.int32, rows.shape, 1) < count
    shift, mask = log2(tiles), tiles - 1
    chunk = rows >> shift
    lanes = group * ring.n_row * tiles
    down = ((chunk >> log2(group)) << shift) + (rows & mask)
    across = (chunk & (group - 1)) * (ring.n_row * tiles) + cols
    table = cross_one_hot(one_hot(ring.n_col // group * tiles, down), one_hot(lanes, across, live))
    near, far = rows - ring.col * tiles, cols - ring.row * tiles
    upper = cross_one_hot(one_hot(tiles, near), one_hot(TILE, far, live))
    lower = cross_one_hot(one_hot(tiles, far, live), one_hot(TILE, near))
    eye = lax.broadcasted_iota(jnp.int32, upper.shape, 0) == lax.broadcasted_iota(
        jnp.int32, upper.shape, 1
    )
    return table, upper + lower + jnp.where(eye, 1.0, 0.0)


def cross_one_hot(former, latter):
    return lax.dot_general(former, latter, (((1,), (1,)), ((), ())), preferred_element_type=F32)


def gather_kernel(
    n_row, n_col, direction, positions, tile_pairs, count, dirs, places, tables, own_table, *sems
):
    ring = Ring(n_row, n_col)
    cover, holders = cover_of(n_row, n_col), holders_of(n_row, n_col)
    tiles = direction.shape[1] // TILE
    group = group_of(n_row, n_col, tiles)
    me = ring.flat((ring.row, ring.col))
    dirs[0] = direction[...].astype(BF16)
    places[0] = positions[...]
    table, own = pattern(ring, tiles, group, tile_pairs, count[0])
    tables[me] = table.reshape(tables.shape[1:]).astype(BF16)
    own_table[...] = own
    ring.greet()
    copies = []
    for k, offset in enumerate(holders):
        place = ring.minus(offset)
        copies.append(remote(tables.at[me], tables.at[me], sems[0].at[k], sems[1].at[k], place))
    for s, offset in enumerate(cover[1:], 1):
        place = ring.minus(offset)
        copies.append(remote(places.at[0], places.at[s], sems[2].at[s], sems[3].at[s], place))
        copies.append(remote(dirs.at[0], dirs.at[s], sems[4].at[s], sems[5].at[s], place))
    for copy in copies:
        copy.start()
    for k, offset in enumerate(holders):
        origin = ring.plus(offset)
        at = tables.at[ring.flat(origin)]
        remote(at, at, sems[0].at[k], sems[1].at[k], origin).wait_recv()
    for s, offset in enumerate(cover[1:], 1):
        origin = ring.plus(offset)
        remote(places.at[0], places.at[s], sems[2].at[s], sems[3].at[s], origin).wait_recv()
        remote(dirs.at[0], dirs.at[s], sems[4].at[s], sems[5].at[s], origin).wait_recv()
    for copy in copies:
        copy.wait_send()


def kernel_of(differ_x, differ_y):
    square = (differ_x * differ_x + differ_y * differ_y).astype(F32)
    square = jnp.minimum(jnp.maximum(square, 1e-20), SCALE * SCALE)
    quad = square * lax.rsqrt(square)
    remain = SCALE - quad
    remain = remain * remain
    return (remain * remain * (quad + 1.0)).astype(BF16)


def times_transposed(vectors, block):
    return lax.dot_general(
        vectors, block, (((1,), (1,)), ((), ())), preferred_element_type=F32
    )


def spread_places(slot, places, near_x, near_y):
    pair = places[slot].astype(F32) * SCALE
    points = pair.shape[1]
    side = lax.broadcasted_iota(jnp.int32, (2, 2 * TILE), 1) // TILE
    pick_side = jnp.where(side == lax.broadcasted_iota(jnp.int32, side.shape, 0), 1.0, 0.0)
    both = lax.dot_general(
        pair.astype(BF16),
        pick_side.astype(BF16),
        (((0,), (0,)), ((), ())),
        preferred_element_type=F32,
    ).astype(BF16)
    near_x[slot] = both[:, :TILE]
    near_y[slot] = both[:, TILE:]


def set_far(slot, mask, places, widen, far_x, far_y):
    pair = places[slot].astype(F32) * SCALE
    on = jnp.dot(mask.astype(BF16), widen[...], preferred_element_type=F32)
    x = (pair[0:1] + FAR_AWAY * (1.0 - on)).astype(BF16)
    for a in range(mask.shape[0]):
        far_x[a] = x[a : a + 1]
    far_y[...] = pair[1:2].astype(BF16)


def block_of(slot, base, tile_row, j, near_x, near_y, far_x, far_y):
    rows = []
    for a in range(2):
        at = pl.ds(pl.multiple_of(base + a * TILE, TILE), TILE)
        x, y = near_x[slot, at, :], near_y[slot, at, :]
        row = []
        for b in range(2):
            across = pl.ds(j * BLOCK + b * TILE, TILE)
            row.append(kernel_of(x - far_x[tile_row + a, :, across], y - far_y[:, across]))
        rows.append(jnp.concatenate(row, axis=1))
    return jnp.concatenate(rows, axis=0)


def pair_kernel(
    n_row, n_col, dirs, places, tables, own_table, parts, own, acc, near_x, near_y, far_x, far_y, widen
):
    ring = Ring(n_row, n_col)
    cover, units = cover_of(n_row, n_col), units_of(n_row, n_col)
    slots, probes, points = dirs.shape
    tiles, blocks = points // TILE, points // BLOCK
    group = group_of(n_row, n_col, tiles)
    scale = AMPLITUDE / 256.0
    acc[...] = jnp.zeros_like(acc)
    lane = lax.broadcasted_iota(jnp.int32, widen.shape, 1) >> log2(TILE)
    widen[...] = jnp.where(lane == lax.broadcasted_iota(jnp.int32, widen.shape, 0), 1.0, 0.0).astype(
        BF16
    )

    @pl.loop(0, slots)
    def _(slot):
        spread_places(slot, places, near_x, near_y)

    set_far(0, own_table[...], places, widen, far_x, far_y)

    @pl.loop(0, blocks)
    def _(i):
        base = pl.multiple_of(i * BLOCK, BLOCK)
        total = jnp.zeros((probes, BLOCK), F32)
        for j in range(blocks):
            block = block_of(0, base, 2 * i, j, near_x, near_y, far_x, far_y)
            total += times_transposed(dirs[0, :, j * BLOCK : (j + 1) * BLOCK], block)
        acc[0, :, pl.ds(base, BLOCK)] += total

    rows_of, cols_of = [o[0] for o in cover], [o[1] for o in cover]

    @pl.loop(0, len(units))
    def _(t):
        i, j = pick(t, [u[0] for u in units]), pick(t, [u[1] for u in units])
        row_i, col_i = ring.plus((pick(i, rows_of), pick(i, cols_of)))
        row_j, col_j = ring.plus((pick(j, rows_of), pick(j, cols_of)))
        swap = (row_i * n_col + col_i - row_j * n_col - col_j + n_row * n_col) // (n_row * n_col)
        low, high = i + swap * (j - i), j + swap * (i - j)
        row_low = row_i + swap * (row_j - row_i)
        row_high = row_j + swap * (row_i - row_j)
        col_low = col_i + swap * (col_j - col_i)
        col_high = col_j + swap * (col_i - col_j)
        table = tables[row_low * n_col + col_high, col_low // group].astype(F32)
        lanes = table.shape[1]
        start = (col_low % group) * (n_row * tiles) + row_high * tiles
        mask = pltpu.roll(table, lax.rem(lanes - start, lanes), 1)
        set_far(high, mask[:, :TILE], places, widen, far_x, far_y)
        half = blocks // 2
        first = swap * half
        forward = [None] * half
        backward = [None] * blocks
        for a in range(half):
            base = pl.multiple_of((first + a) * BLOCK, BLOCK)
            near_vec = dirs[low, :, pl.ds(base, BLOCK)]
            for b in range(blocks):
                block = block_of(low, base, 2 * (first + a), b, near_x, near_y, far_x, far_y)
                ahead = times_transposed(dirs[high, :, b * BLOCK : (b + 1) * BLOCK], block)
                back = jnp.dot(near_vec, block, preferred_element_type=F32)
                forward[a] = ahead if b == 0 else forward[a] + ahead
                backward[b] = back if a == 0 else backward[b] + back
        for a in range(half):
            base = pl.multiple_of((first + a) * BLOCK, BLOCK)
            acc[low, :, pl.ds(base, BLOCK)] += forward[a]
        for b in range(blocks):
            acc[high, :, b * BLOCK : (b + 1) * BLOCK] += backward[b]

    own[...] = scale * acc[0]
    for s in range(1, slots):
        parts[s - 1] = (scale * acc[s]).astype(BF16)


class Exchange:
    def __init__(self, axis, size, source, landing, send_sem, recv_sem):
        self.axis, self.size, self.source, self.landing = axis, size, source, landing
        self.send_sem, self.recv_sem = send_sem, recv_sem
        self.me = lax.axis_index(axis)

    def copy(self, k, source, slot, peer):
        return pltpu.make_async_remote_copy(
            src_ref=source,
            dst_ref=self.landing.at[slot],
            send_sem=self.send_sem.at[k],
            recv_sem=self.recv_sem.at[k],
            device_id={self.axis: peer},
            device_id_type=MESH,
        )

    def outgoing(self, k):
        peer = lax.rem(self.me + k, self.size)
        return self.copy(k, self.source, self.me, peer)

    def start(self):
        for k in range(1, self.size):
            self.outgoing(k).start()

    def wait_recv(self):
        for k in range(1, self.size):
            origin = lax.rem(self.me + self.size - k, self.size)
            self.copy(k, self.landing.at[origin], origin, origin).wait_recv()

    def wait_send(self):
        for k in range(1, self.size):
            self.outgoing(k).wait_send()


def image_kernel(
    n_row,
    n_col,
    parts,
    own,
    direction,
    residual,
    applied,
    gram,
    land,
    gram_own,
    gram_half,
    gram_col,
    gram_row,
    *sems,
):
    ring = Ring(n_row, n_col)
    cover = cover_of(n_row, n_col)
    ring.greet()
    sends = []
    for s, offset in enumerate(cover[1:], 1):
        place = ring.plus(offset)
        sends.append(
            remote(parts.at[s - 1], land.at[s - 1], sems[0].at[s - 1], sems[1].at[s - 1], place)
        )
    for copy in sends:
        copy.start()
    total = own[...] + NUGGET * direction[...]
    for s, offset in enumerate(cover[1:], 1):
        place = ring.minus(offset)
        remote(
            parts.at[s - 1], land.at[s - 1], sems[0].at[s - 1], sems[1].at[s - 1], place
        ).wait_recv()
        total += land[s - 1].astype(F32)
    image = total
    applied[...] = image
    left = jnp.concatenate([image, residual[...]], axis=0)
    right = jnp.concatenate([left, direction[...]], axis=0)
    product = cross_gram_matrix(left, right)
    lanes = gram_own.shape[1] - product.shape[1]
    gram_own[...] = jnp.concatenate([product, jnp.zeros((product.shape[0], lanes), F32)], axis=1)
    gram_over_col = Exchange("col", n_col, gram_own, gram_col, sems[2], sems[3])
    gram_over_col.start()
    gram_over_col.wait_recv()
    half = gram_own[...]
    for k in range(1, n_col):
        half += gram_col[lax.rem(ring.col + k, n_col)]
    gram_half[...] = half
    gram_over_row = Exchange("row", n_row, gram_half, gram_row, sems[4], sems[5])
    gram_over_row.start()
    gram_over_row.wait_recv()
    whole = gram_half[...]
    for k in range(1, n_row):
        whole += gram_row[lax.rem(ring.row + k, n_row)]
    gram[...] = whole
    for copy in sends:
        copy.wait_send()
    gram_over_col.wait_send()
    gram_over_row.wait_send()


def on_device(solution_field, residual, direction, positions, tile_pairs, pair_count):
    probes, points = direction.shape
    n_row, n_col = lax.axis_size("row"), lax.axis_size("col")
    cover, holders = cover_of(n_row, n_col), holders_of(n_row, n_col)
    slots, tiles = len(cover), points // TILE
    group = group_of(n_row, n_col, tiles)
    lanes = group * n_row * tiles
    vmem = pl.BlockSpec(memory_space=pltpu.VMEM)
    smem = pl.BlockSpec(memory_space=pltpu.SMEM)
    dma = pltpu.SemaphoreType.DMA
    dirs, places, tables, own_table = pl.pallas_call(
        functools.partial(gather_kernel, n_row, n_col),
        out_shape=(
            jax.ShapeDtypeStruct((slots, probes, points), BF16),
            jax.ShapeDtypeStruct((slots, 2, points), BF16),
            jax.ShapeDtypeStruct((n_row * n_col, n_col // group, tiles, lanes), BF16),
            jax.ShapeDtypeStruct((tiles, TILE), F32),
        ),
        in_specs=[vmem, vmem, vmem, smem],
        out_specs=(vmem,) * 4,
        scratch_shapes=[dma((len(holders),))] * 2 + [dma((slots,))] * 4,
        compiler_params=pltpu.CompilerParams(collective_id=0, has_side_effects=True),
        name="gather",
    )(direction, positions, tile_pairs, pair_count)
    parts, own = pl.pallas_call(
        functools.partial(pair_kernel, n_row, n_col),
        out_shape=(
            jax.ShapeDtypeStruct((slots - 1, probes, points), BF16),
            jax.ShapeDtypeStruct((probes, points), F32),
        ),
        in_specs=[vmem] * 4,
        out_specs=(vmem,) * 2,
        scratch_shapes=[
            pltpu.VMEM((slots, probes, points), F32),
            pltpu.VMEM((slots, points, TILE), BF16),
            pltpu.VMEM((slots, points, TILE), BF16),
            pltpu.VMEM((tiles, 1, points), BF16),
            pltpu.VMEM((1, points), BF16),
            pltpu.VMEM((TILE, points), BF16),
        ],
        name="pairs",
    )(dirs, places, tables, own_table)
    applied, gram = pl.pallas_call(
        functools.partial(image_kernel, n_row, n_col),
        out_shape=(
            jax.ShapeDtypeStruct((probes, points), F32),
            jax.ShapeDtypeStruct((2 * probes, TILE), F32),
        ),
        in_specs=[vmem] * 4,
        out_specs=(vmem, vmem),
        scratch_shapes=[
            pltpu.VMEM((slots - 1, probes, points), BF16),
            pltpu.VMEM((2 * probes, TILE), F32),
            pltpu.VMEM((2 * probes, TILE), F32),
            pltpu.VMEM((n_col, 2 * probes, TILE), F32),
            pltpu.VMEM((n_row, 2 * probes, TILE), F32),
            dma((slots - 1,)),
            dma((slots - 1,)),
            dma((n_col,)),
            dma((n_col,)),
            dma((n_row,)),
            dma((n_row,)),
        ],
        compiler_params=pltpu.CompilerParams(collective_id=1, has_side_effects=True),
        name="image",
    )(parts, own, direction, residual)
    square, image_resid = gram[:probes, :probes], gram[:probes, probes : 2 * probes]
    norm_old = gram[probes:, probes : 2 * probes]
    curvature = gram[:probes, 2 * probes : 3 * probes].T
    crossing = gram[probes:, 2 * probes : 3 * probes].T
    step_size = symmetric_solve(curvature, crossing)
    residual_next = residual - apply_left(step_size, applied)
    shifted = jnp.dot(step_size.T, image_resid, precision=HIGHEST)
    quadratic = jnp.dot(
        step_size.T, jnp.dot(square, step_size, precision=HIGHEST), precision=HIGHEST
    )
    norm_new = norm_old - shifted - shifted.T + quadratic
    solution_next = solution_field + apply_left(step_size, direction)
    mix_weight = symmetric_solve(norm_old, norm_new)
    direction_next = residual_next + apply_left(mix_weight, direction)
    return (solution_next, residual_next, direction_next)


def solution(mesh):
    whole = P(None, ("row", "col"))
    return jax.shard_map(
        on_device,
        mesh=mesh,
        in_specs=(whole, whole, whole, whole, whole, P(("row", "col"))),
        out_specs=(whole, whole, whole),
        check_vma=False,
    )
```

time: 196 us -> 119 us (0.61)
  Pallas kernels: 170 us -> 99 us
  local copies, waits for them, and re-layouts: 4.76 us -> 1.54 us
  other arithmetic: 15.6 us -> 13.5 us
    pallas_call x1, Pallas kernels: 120 us -> 54.8 us  [on_device(): pl.pallas_call(functools.partial(pair_kernel, n_row, n_col), out_shape=(j...]
    pallas_call x1, Pallas kernels: 29.6 us -> 23.6 us  [on_device(): pl.pallas_call(functools.partial(image_kernel, n_row, n_col), out_shape=(...]
    transpose x2 -> x0, local copies, waits for them, and re-layouts: 2.26 us -> none  [on_device(): near = row_pack[:, probes:].transpose(0, 2, 1)]
where the time goes in v1:
time: 119 us
  Pallas kernels  99 us (83%)
  other arithmetic  13.5 us (11%)
  matrix products  3.59 us (3%)
  local copies, waits for them, and re-layouts  1.54 us (1%)
  between operations  1.43 us (1%)
    pallas_call x1, Pallas kernels, on_device(): pl.pallas_call(functools.partial(pair_kernel, n_row, n_col), out_shape=(j...  54.8 us
    pallas_call x1, Pallas kernels, on_device(): pl.pallas_call(functools.partial(image_kernel, n_row, n_col), out_shape=(...  23.6 us
    pallas_call x1, Pallas kernels, on_device(): pl.pallas_call(functools.partial(gather_kernel, n_row, n_col), out_shape=...  20.7 us
    another operation x6, other arithmetic, symmetric_solve(): factor = jnp.linalg.cholesky(balanced)  7.2 us
    another operation x4, other arithmetic, symmetric_solve(): lax.linalg.triangular_solve(factor, middle, left_side=True, lower=True, t...  6.17 us

profile of v1, /device:TPU:0, one launch (start us, length us, event | category | flops | bytes accessed | tf_op | source)
XLA Modules:
  0.0 119.0 jit_solution(15152533542378531599)
XLA Ops:
  1.3 20.7 %gather.1 = (bf16[7,32,1024]{2,1,0:T(8,128)(2,1)}, bf16[7,2,1024]{2,1,0:T(2,128)(2,1)}, bf16[32,2,8,128]{3,2,1,0:T(8,128)(2,1)}, f32[8,128]{1,0:T(8,128)}) custom-call(f32[32,1024]{1,0:T(8,128)} %direction.3, bf16[2,1024]{1,0:T(2,128)(2,1)} %positions.1, s32[2,1536]{1,0:T(2,128)} %tile_pairs.1, s32[1]{0:T(128)S(6)} %copy.15.count), custom_call_target="tpu_custom_call" | custom-call | tf_op jit(solution)/shard_map/gather/pallas_call | solution.py:457
  21.9 54.8 %pairs.1 = (bf16[6,32,1024]{2,1,0:T(8,128)(2,1)}, f32[32,1024]{1,0:T(8,128)}) custom-call(bf16[7,32,1024]{2,1,0:T(8,128)(2,1)} %get-tuple-element.14.dirs, bf16[7,2,1024]{2,1,0:T(2,128)(2,1)} %get-tuple-element.15.places, bf16[32,2,8,128]{3,2,1,0:T(8,128)(2,1)} %get-tuple-element.16.tables, f32[8,128]{1,0:T(8,128)} %get-tuple-element.17.own_table), custom_call_target="tpu_custom_call" | custom-call | tf_op jit(solution)/shard_map/pairs/pallas_call | solution.py:471
  76.8 23.6 %image.1 = (f32[32,1024]{1,0:T(8,128)}, f32[64,128]{1,0:T(8,128)}) custom-call(bf16[6,32,1024]{2,1,0:T(8,128)(2,1)} %get-tuple-element.18.parts, f32[32,1024]{1,0:T(8,128)} %get-tuple-element.19.own, f32[32,1024]{1,0:T(8,128)} %direction.3, f32[32,1024]{1,0:T(8,128)} %residual.1), custom_call_target="tpu_custom_call" | custom-call | tf_op jit(solution)/shard_map/image/pallas_call | solution.py:489
  100.3 0.0 copy-start.2
  100.3 0.9 slice.25
  101.2 0.1 copy.12
  101.3 0.0 copy-done.2
  101.3 0.1 fusion.7
  101.3 0.1 copy.13
  101.4 2.9 %cholesky.55 = f32[32,32]{1,0:T(8,128)S(1)} custom-call(f32[32,32]{1,0:T(8,128)S(1)} %fusion.6), custom_call_target="Cholesky" | custom-call | tf_op jit(solution)/shard_map/jit(cholesky)/cholesky | solution.py:36
  104.4 0.6 compare_reduce_fusion
  105.0 0.7 fusion.1
  105.7 2.4 %custom-call.13 = f32[1,32,32]{1,2,0:T(8,128)S(1)} custom-call(f32[1,32,32]{2,1,0:T(8,128)S(1)} %fusion.1), custom_call_target="InvertDiagBlocksLowerTriangular" | custom-call | tf_op jit(solution)/shard_map/triangular_solve/custom-call.2 | solution.py:38
  108.1 0.1 copy.9
  108.2 0.1 copy.10
  108.3 0.0 copy-start.3
  108.3 0.0 copy-start.5
  108.3 0.1 copy.11
  108.4 2.9 %cholesky.44 = f32[32,32]{1,0:T(8,128)S(1)} custom-call(f32[32,32]{1,0:T(8,128)S(1)} %fusion.13), custom_call_target="Cholesky" | custom-call | tf_op jit(solution)/shard_map/jit(cholesky)/cholesky | solution.py:36
  111.4 0.6 compare_reduce_fusion.1
  112.0 0.7 fusion
  112.7 2.4 %custom-call.11 = f32[1,32,32]{1,2,0:T(8,128)S(1)} custom-call(f32[1,32,32]{2,1,0:T(8,128)S(1)} %fusion), custom_call_target="InvertDiagBlocksLowerTriangular" | custom-call | tf_op jit(solution)/shard_map/triangular_solve/custom-call.2 | solution.py:38
  115.1 0.3 fusion.8
  115.4 0.1 fusion.11
  115.5 0.0 copy-done.3
  115.5 0.0 copy-done.5
  115.5 0.3 convolution_subtract_fusion
  115.9 0.0 copy-start.1
  115.9 0.2 fusion.16
  116.1 0.1 copy.14
  116.2 0.0 copy-start
  116.2 0.1 fusion.14
  116.3 0.2 convolution_add_fusion.2
  116.6 0.2 fusion.2
  116.8 0.1 fusion.4
  116.9 0.0 copy-done.1
  116.9 0.2 copy-done
  117.1 0.0 copy-start.4
  117.1 1.0 convolution_add_fusion
  118.1 0.0 copy-done.4
  118.1 1.0 convolution_add_fusion.1
  (6 shorter events, 0.1 us)
Async XLA Ops:
  100.3 0.9 copy-start.2
  108.3 7.2 %copy-start.3 = (f32[32,1024]{1,0:T(8,128)S(1)}, f32[32,1024]{1,0:T(8,128)}, u32[]{:S(2)}) copy-start(f32[32,1024]{1,0:T(8,128)} %residual.1) | copy-start | bytes 393220
  108.3 7.2 %copy-start.5 = (f32[32,1024]{1,0:T(8,128)S(1)}, f32[32,1024]{1,0:T(8,128)}, u32[]{:S(2)}) copy-start(f32[32,1024]{1,0:T(8,128)} %get-tuple-element.21) | copy-start | bytes 393220
  115.9 1.1 copy-start.1
  116.2 0.9 copy-start
  117.1 1.0 copy-start.4

commit v2 on v1

--- a/solution.py
+++ b/solution.py
@@ -189,42 +189,6 @@
     return lax.dot_general(former, latter, (((1,), (1,)), ((), ())), preferred_element_type=F32)
 
 
-def gather_kernel(
-    n_row, n_col, direction, positions, tile_pairs, count, dirs, places, tables, own_table, *sems
-):
-    ring = Ring(n_row, n_col)
-    cover, holders = cover_of(n_row, n_col), holders_of(n_row, n_col)
-    tiles = direction.shape[1] // TILE
-    group = group_of(n_row, n_col, tiles)
-    me = ring.flat((ring.row, ring.col))
-    dirs[0] = direction[...].astype(BF16)
-    places[0] = positions[...]
-    table, own = pattern(ring, tiles, group, tile_pairs, count[0])
-    tables[me] = table.reshape(tables.shape[1:]).astype(BF16)
-    own_table[...] = own
-    ring.greet()
-    copies = []
-    for k, offset in enumerate(holders):
-        place = ring.minus(offset)
-        copies.append(remote(tables.at[me], tables.at[me], sems[0].at[k], sems[1].at[k], place))
-    for s, offset in enumerate(cover[1:], 1):
-        place = ring.minus(offset)
-        copies.append(remote(places.at[0], places.at[s], sems[2].at[s], sems[3].at[s], place))
-        copies.append(remote(dirs.at[0], dirs.at[s], sems[4].at[s], sems[5].at[s], place))
-    for copy in copies:
-        copy.start()
-    for k, offset in enumerate(holders):
-        origin = ring.plus(offset)
-        at = tables.at[ring.flat(origin)]
-        remote(at, at, sems[0].at[k], sems[1].at[k], origin).wait_recv()
-    for s, offset in enumerate(cover[1:], 1):
-        origin = ring.plus(offset)
-        remote(places.at[0], places.at[s], sems[2].at[s], sems[3].at[s], origin).wait_recv()
-        remote(dirs.at[0], dirs.at[s], sems[4].at[s], sems[5].at[s], origin).wait_recv()
-    for copy in copies:
-        copy.wait_send()
-
-
 def kernel_of(differ_x, differ_y):
     square = (differ_x * differ_x + differ_y * differ_y).astype(F32)
     square = jnp.minimum(jnp.maximum(square, 1e-20), SCALE * SCALE)
@@ -277,26 +241,116 @@
     return jnp.concatenate(rows, axis=0)
 
 
-def pair_kernel(
-    n_row, n_col, dirs, places, tables, own_table, parts, own, acc, near_x, near_y, far_x, far_y, widen
+def batches_of(n_row, n_col):
+    cover, units = cover_of(n_row, n_col), list(units_of(n_row, n_col))
+    result, waited = [], {0}
+    for slot in range(1, len(cover)):
+        mine = sorted((u for u in units if slot in u), key=lambda u: (sum(u) - slot, u))
+        units = [u for u in units if slot not in u]
+        cut = [u for u in mine if sum(u) - slot <= len(cover) // 2]
+        pieces = [cut, mine[len(cut) :]] if slot == 1 else [mine]
+        pieces = [piece for piece in pieces if piece]
+        for k, piece in enumerate(pieces):
+            need = sorted({s for u in piece for s in u} - waited)
+            waited |= set(need)
+            result.append((need, piece, slot if k == len(pieces) - 1 else None))
+    return result
+
+
+def step_kernel(
+    n_row,
+    n_col,
+    direction,
+    residual,
+    positions,
+    tile_pairs,
+    count,
+    applied,
+    gram,
+    dirs,
+    places,
+    tables,
+    acc,
+    near_x,
+    near_y,
+    far_x,
+    far_y,
+    widen,
+    parts,
+    land,
+    gram_own,
+    gram_half,
+    gram_col,
+    gram_row,
+    *sems,
 ):
     ring = Ring(n_row, n_col)
-    cover, units = cover_of(n_row, n_col), units_of(n_row, n_col)
+    cover, holders = cover_of(n_row, n_col), holders_of(n_row, n_col)
     slots, probes, points = dirs.shape
     tiles, blocks = points // TILE, points // BLOCK
+    half = blocks // 2
     group = group_of(n_row, n_col, tiles)
     scale = AMPLITUDE / 256.0
+    me = ring.flat((ring.row, ring.col))
+
+    dirs[0] = direction[...].astype(BF16)
+    places[0] = positions[...]
+    table, own_table = pattern(ring, tiles, group, tile_pairs, count[0])
+    tables[me] = table.reshape(tables.shape[1:]).astype(BF16)
+    ring.greet()
+    sends = []
+    for s, offset in enumerate(cover[1:], 1):
+        place = ring.minus(offset)
+        sends.append(remote(places.at[0], places.at[s], sems[2].at[s], sems[3].at[s], place))
+    for k, offset in enumerate(holders):
+        place = ring.minus(offset)
+        sends.append(remote(tables.at[me], tables.at[me], sems[0].at[k], sems[1].at[k], place))
+    for s, offset in enumerate(cover[1:], 1):
+        place = ring.minus(offset)
+        sends.append(remote(dirs.at[0], dirs.at[s], sems[4].at[s], sems[5].at[s], place))
+    for copy in sends:
+        copy.start()
+
+    def exchanges(part):
+        base = 8 + 4 * part
+        over_col = Exchange(
+            "col", n_col, gram_own.at[part], gram_col.at[part], sems[base], sems[base + 1]
+        )
+        over_row = Exchange(
+            "row", n_row, gram_half.at[part], gram_row.at[part], sems[base + 2], sems[base + 3]
+        )
+        return over_col, over_row
+
+    def sum_cols(part):
+        total = gram_own[part]
+        for k in range(1, n_col):
+            total += gram_col[part, lax.rem(ring.col + k, n_col)]
+        gram_half[part] = total
+
+    def sum_rows(part):
+        total = gram_half[part]
+        for k in range(1, n_row):
+            total += gram_row[part, lax.rem(ring.row + k, n_row)]
+        gram[part * probes : (part + 1) * probes] = total
+
+    def padded(product, before):
+        widths = (before, TILE - before - product.shape[1])
+        sides = [[jnp.zeros((probes, n), F32)] if n else [] for n in widths]
+        return jnp.concatenate(sides[0] + [product] + sides[1], axis=1)
+
+    early_col, early_row = exchanges(1)
+    late_col, late_row = exchanges(0)
+    sides = jnp.concatenate([residual[...], direction[...]], axis=0)
+    gram_own[1] = padded(cross_gram_matrix(residual[...], sides), probes)
+    early_col.start()
+
     acc[...] = jnp.zeros_like(acc)
     lane = lax.broadcasted_iota(jnp.int32, widen.shape, 1) >> log2(TILE)
     widen[...] = jnp.where(lane == lax.broadcasted_iota(jnp.int32, widen.shape, 0), 1.0, 0.0).astype(
         BF16
     )
-
-    @pl.loop(0, slots)
-    def _(slot):
-        spread_places(slot, places, near_x, near_y)
-
-    set_far(0, own_table[...], places, widen, far_x, far_y)
+    spread_places(0, places, near_x, near_y)
+    set_far(0, own_table, places, widen, far_x, far_y)
 
     @pl.loop(0, blocks)
     def _(i):
@@ -307,11 +361,22 @@
             total += times_transposed(dirs[0, :, j * BLOCK : (j + 1) * BLOCK], block)
         acc[0, :, pl.ds(base, BLOCK)] += total
 
+    for s, offset in enumerate(cover[1:], 1):
+        origin = ring.plus(offset)
+        remote(places.at[0], places.at[s], sems[2].at[s], sems[3].at[s], origin).wait_recv()
+
+    @pl.loop(1, slots)
+    def _(slot):
+        spread_places(slot, places, near_x, near_y)
+
+    for k, offset in enumerate(holders):
+        origin = ring.plus(offset)
+        at = tables.at[ring.flat(origin)]
+        remote(at, at, sems[0].at[k], sems[1].at[k], origin).wait_recv()
+
     rows_of, cols_of = [o[0] for o in cover], [o[1] for o in cover]
 
-    @pl.loop(0, len(units))
-    def _(t):
-        i, j = pick(t, [u[0] for u in units]), pick(t, [u[1] for u in units])
+    def unit(i, j):
         row_i, col_i = ring.plus((pick(i, rows_of), pick(i, cols_of)))
         row_j, col_j = ring.plus((pick(j, rows_of), pick(j, cols_of)))
         swap = (row_i * n_col + col_i - row_j * n_col - col_j + n_row * n_col) // (n_row * n_col)
@@ -325,7 +390,6 @@
         start = (col_low % group) * (n_row * tiles) + row_high * tiles
         mask = pltpu.roll(table, lax.rem(lanes - start, lanes), 1)
         set_far(high, mask[:, :TILE], places, widen, far_x, far_y)
-        half = blocks // 2
         first = swap * half
         forward = [None] * half
         backward = [None] * blocks
@@ -344,9 +408,46 @@
         for b in range(blocks):
             acc[high, :, b * BLOCK : (b + 1) * BLOCK] += backward[b]
 
-    own[...] = scale * acc[0]
-    for s in range(1, slots):
-        parts[s - 1] = (scale * acc[s]).astype(BF16)
+    for k, (need, units, complete) in enumerate(batches_of(n_row, n_col)):
+        for s in need:
+            origin = ring.plus(cover[s])
+            remote(dirs.at[0], dirs.at[s], sems[4].at[s], sems[5].at[s], origin).wait_recv()
+
+        @pl.loop(0, len(units))
+        def _(t):
+            unit(pick(t, [u[0] for u in units]), pick(t, [u[1] for u in units]))
+
+        if k == 0:
+            early_col.wait_recv()
+            sum_cols(1)
+            early_row.start()
+        if k == 1:
+            early_row.wait_recv()
+            sum_rows(1)
+        if complete is not None:
+            s = complete - 1
+            parts[s] = (scale * acc[complete]).astype(BF16)
+            copy = remote(
+                parts.at[s], land.at[s], sems[6].at[s], sems[7].at[s], ring.plus(cover[complete])
+            )
+            copy.start()
+            sends.append(copy)
+
+    image = scale * acc[0] + NUGGET * direction[...]
+    for s, offset in enumerate(cover[1:]):
+        origin = ring.minus(offset)
+        remote(parts.at[s], land.at[s], sems[6].at[s], sems[7].at[s], origin).wait_recv()
+        image += land[s].astype(F32)
+    applied[...] = image
+    gram_own[0] = padded(cross_gram_matrix(image, jnp.concatenate([image, sides], axis=0)), 0)
+    late_col.start()
+    late_col.wait_recv()
+    sum_cols(0)
+    late_row.start()
+    late_row.wait_recv()
+    sum_rows(0)
+    for copy in sends + [early_col, early_row, late_col, late_row]:
+        copy.wait_send()
 
 
 class Exchange:
@@ -381,67 +482,6 @@
     def wait_send(self):
         for k in range(1, self.size):
             self.outgoing(k).wait_send()
-
-
-def image_kernel(
-    n_row,
-    n_col,
-    parts,
-    own,
-    direction,
-    residual,
-    applied,
-    gram,
-    land,
-    gram_own,
-    gram_half,
-    gram_col,
-    gram_row,
-    *sems,
-):
-    ring = Ring(n_row, n_col)
-    cover = cover_of(n_row, n_col)
-    ring.greet()
-    sends = []
-    for s, offset in enumerate(cover[1:], 1):
-        place = ring.plus(offset)
-        sends.append(
-            remote(parts.at[s - 1], land.at[s - 1], sems[0].at[s - 1], sems[1].at[s - 1], place)
-        )
-    for copy in sends:
-        copy.start()
-    total = own[...] + NUGGET * direction[...]
-    for s, offset in enumerate(cover[1:], 1):
-        place = ring.minus(offset)
-        remote(
-            parts.at[s - 1], land.at[s - 1], sems[0].at[s - 1], sems[1].at[s - 1], place
-        ).wait_recv()
-        total += land[s - 1].astype(F32)
-    image = total
-    applied[...] = image
-    left = jnp.concatenate([image, residual[...]], axis=0)
-    right = jnp.concatenate([left, direction[...]], axis=0)
-    product = cross_gram_matrix(left, right)
-    lanes = gram_own.shape[1] - product.shape[1]
-    gram_own[...] = jnp.concatenate([product, jnp.zeros((product.shape[0], lanes), F32)], axis=1)
-    gram_over_col = Exchange("col", n_col, gram_own, gram_col, sems[2], sems[3])
-    gram_over_col.start()
-    gram_over_col.wait_recv()
-    half = gram_own[...]
-    for k in range(1, n_col):
-        half += gram_col[lax.rem(ring.col + k, n_col)]
-    gram_half[...] = half
-    gram_over_row = Exchange("row", n_row, gram_half, gram_row, sems[4], sems[5])
-    gram_over_row.start()
-    gram_over_row.wait_recv()
-    whole = gram_half[...]
-    for k in range(1, n_row):
-        whole += gram_row[lax.rem(ring.row + k, n_row)]
-    gram[...] = whole
-    for copy in sends:
-        copy.wait_send()
-    gram_over_col.wait_send()
-    gram_over_row.wait_send()
 
 
 def on_device(solution_field, residual, direction, positions, tile_pairs, pair_count):
@@ -454,62 +494,38 @@
     vmem = pl.BlockSpec(memory_space=pltpu.VMEM)
     smem = pl.BlockSpec(memory_space=pltpu.SMEM)
     dma = pltpu.SemaphoreType.DMA
-    dirs, places, tables, own_table = pl.pallas_call(
-        functools.partial(gather_kernel, n_row, n_col),
+    applied, gram = pl.pallas_call(
+        functools.partial(step_kernel, n_row, n_col),
         out_shape=(
-            jax.ShapeDtypeStruct((slots, probes, points), BF16),
-            jax.ShapeDtypeStruct((slots, 2, points), BF16),
-            jax.ShapeDtypeStruct((n_row * n_col, n_col // group, tiles, lanes), BF16),
-            jax.ShapeDtypeStruct((tiles, TILE), F32),
+            jax.ShapeDtypeStruct((probes, points), F32),
+            jax.ShapeDtypeStruct((2 * probes, TILE), F32),
         ),
-        in_specs=[vmem, vmem, vmem, smem],
-        out_specs=(vmem,) * 4,
-        scratch_shapes=[dma((len(holders),))] * 2 + [dma((slots,))] * 4,
-        compiler_params=pltpu.CompilerParams(collective_id=0, has_side_effects=True),
-        name="gather",
-    )(direction, positions, tile_pairs, pair_count)
-    parts, own = pl.pallas_call(
-        functools.partial(pair_kernel, n_row, n_col),
-        out_shape=(
-            jax.ShapeDtypeStruct((slots - 1, probes, points), BF16),
-            jax.ShapeDtypeStruct((probes, points), F32),
-        ),
-        in_specs=[vmem] * 4,
-        out_specs=(vmem,) * 2,
+        in_specs=[vmem] * 4 + [smem],
+        out_specs=(vmem, vmem),
         scratch_shapes=[
+            pltpu.VMEM((slots, probes, points), BF16),
+            pltpu.VMEM((slots, 2, points), BF16),
+            pltpu.VMEM((n_row * n_col, n_col // group, tiles, lanes), BF16),
             pltpu.VMEM((slots, probes, points), F32),
             pltpu.VMEM((slots, points, TILE), BF16),
             pltpu.VMEM((slots, points, TILE), BF16),
             pltpu.VMEM((tiles, 1, points), BF16),
             pltpu.VMEM((1, points), BF16),
             pltpu.VMEM((TILE, points), BF16),
-        ],
-        name="pairs",
-    )(dirs, places, tables, own_table)
-    applied, gram = pl.pallas_call(
-        functools.partial(image_kernel, n_row, n_col),
-        out_shape=(
-            jax.ShapeDtypeStruct((probes, points), F32),
-            jax.ShapeDtypeStruct((2 * probes, TILE), F32),
-        ),
-        in_specs=[vmem] * 4,
-        out_specs=(vmem, vmem),
-        scratch_shapes=[
             pltpu.VMEM((slots - 1, probes, points), BF16),
-            pltpu.VMEM((2 * probes, TILE), F32),
-            pltpu.VMEM((2 * probes, TILE), F32),
-            pltpu.VMEM((n_col, 2 * probes, TILE), F32),
-            pltpu.VMEM((n_row, 2 * probes, TILE), F32),
-            dma((slots - 1,)),
-            dma((slots - 1,)),
-            dma((n_col,)),
-            dma((n_col,)),
-            dma((n_row,)),
-            dma((n_row,)),
-        ],
-        compiler_params=pltpu.CompilerParams(collective_id=1, has_side_effects=True),
-        name="image",
-    )(parts, own, direction, residual)
+            pltpu.VMEM((slots - 1, probes, points), BF16),
+            pltpu.VMEM((2, probes, TILE), F32),
+            pltpu.VMEM((2, probes, TILE), F32),
+            pltpu.VMEM((2, n_col, probes, TILE), F32),
+            pltpu.VMEM((2, n_row, probes, TILE), F32),
+        ]
+        + [dma((len(holders),))] * 2
+        + [dma((slots,))] * 4
+        + [dma((slots - 1,))] * 2
+        + [dma((n_col,)), dma((n_col,)), dma((n_row,)), dma((n_row,))] * 2,
+        compiler_params=pltpu.CompilerParams(collective_id=0, has_side_effects=True),
+        name="step",
+    )(direction, residual, positions, tile_pairs, pair_count)
     square, image_resid = gram[:probes, :probes], gram[:probes, probes : 2 * probes]
     norm_old = gram[probes:, probes : 2 * probes]
     curvature = gram[:probes, 2 * probes : 3 * probes].T

time: 119 us -> 97.7 us (0.82)
  Pallas kernels: 99 us -> 77.4 us
    pallas_call x3 -> x1, Pallas kernels: 99 us -> 77.4 us  [on_device(): pl.pallas_call(functools.partial(step_kernel, n_row, n_col), out_shape=(j...]
where the time goes in v2:
time: 97.7 us; the launch traced here: 97.4 us
  Pallas kernels  77.4 us (79%)
  other arithmetic  13.5 us (14%)
  matrix products  3.59 us (4%)
  local copies, waits for them, and re-layouts  1.54 us (2%)
  between operations  1.42 us (1%)
    pallas_call x1, Pallas kernels, on_device(): pl.pallas_call(functools.partial(step_kernel, n_row, n_col), out_shape=(j...  77.4 us
    another operation x6, other arithmetic, symmetric_solve(): factor = jnp.linalg.cholesky(balanced)  7.2 us
    another operation x4, other arithmetic, symmetric_solve(): lax.linalg.triangular_solve(factor, middle, left_side=True, lower=True, t...  6.17 us
    dot_general x3, matrix products, apply_left(): return jnp.dot(matrix.T, vectors, precision=HIGHEST)  2.26 us

profile of v2, /device:TPU:0, one launch (start us, length us, event | category | flops | bytes accessed | tf_op | source)
XLA Modules:
  0.0 97.4 jit_solution(9029984281459972836)
XLA Ops:
  1.3 77.4 %step.1 = (f32[32,1024]{1,0:T(8,128)}, f32[64,128]{1,0:T(8,128)}) custom-call(f32[32,1024]{1,0:T(8,128)} %direction.1, f32[32,1024]{1,0:T(8,128)} %residual.1, bf16[2,1024]{1,0:T(2,128)(2,1)} %positions.1, s32[2,1536]{1,0:T(2,128)} %tile_pairs.1, s32[1]{0:T(128)S(6)} %copy.15.count), custom_call_target="tpu_custom_call" | custom-call | tf_op jit(solution)/shard_map/step/pallas_call | solution.py:497
  78.7 0.0 copy-start.2
  78.7 0.9 slice.25
  79.6 0.1 copy.12
  79.7 0.0 copy-done.2
  79.7 0.1 fusion.7
  79.7 0.1 copy.13
  79.8 2.9 %cholesky.55 = f32[32,32]{1,0:T(8,128)S(1)} custom-call(f32[32,32]{1,0:T(8,128)S(1)} %fusion.6), custom_call_target="Cholesky" | custom-call | tf_op jit(solution)/shard_map/jit(cholesky)/cholesky | solution.py:36
  82.8 0.6 compare_reduce_fusion
  83.4 0.7 fusion.1
  84.1 2.4 %custom-call.13 = f32[1,32,32]{1,2,0:T(8,128)S(1)} custom-call(f32[1,32,32]{2,1,0:T(8,128)S(1)} %fusion.1), custom_call_target="InvertDiagBlocksLowerTriangular" | custom-call | tf_op jit(solution)/shard_map/triangular_solve/custom-call.2 | solution.py:38
  86.5 0.1 copy.9
  86.6 0.1 copy.10
  86.7 0.0 copy-start.3
  86.7 0.0 copy-start.5
  86.7 0.1 copy.11
  86.8 2.9 %cholesky.44 = f32[32,32]{1,0:T(8,128)S(1)} custom-call(f32[32,32]{1,0:T(8,128)S(1)} %fusion.13), custom_call_target="Cholesky" | custom-call | tf_op jit(solution)/shard_map/jit(cholesky)/cholesky | solution.py:36
  89.8 0.6 compare_reduce_fusion.1
  90.4 0.7 fusion
  91.1 2.4 %custom-call.11 = f32[1,32,32]{1,2,0:T(8,128)S(1)} custom-call(f32[1,32,32]{2,1,0:T(8,128)S(1)} %fusion), custom_call_target="InvertDiagBlocksLowerTriangular" | custom-call | tf_op jit(solution)/shard_map/triangular_solve/custom-call.2 | solution.py:38
  93.5 0.3 fusion.8
  93.8 0.1 fusion.11
  93.9 0.0 copy-done.3
  93.9 0.0 copy-done.5
  93.9 0.3 convolution_subtract_fusion
  94.3 0.0 copy-start.1
  94.3 0.2 fusion.16
  94.5 0.1 copy.14
  94.6 0.0 copy-start
  94.6 0.1 fusion.14
  94.7 0.2 convolution_add_fusion.2
  95.0 0.2 fusion.2
  95.2 0.1 fusion.4
  95.3 0.0 copy-done.1
  95.3 0.2 copy-done
  95.5 0.0 copy-start.4
  95.5 1.0 convolution_add_fusion
  96.5 0.0 copy-done.4
  96.5 1.0 convolution_add_fusion.1
  (6 shorter events, 0.1 us)
Async XLA Ops:
  78.7 0.9 copy-start.2
  86.7 7.2 %copy-start.3 = (f32[32,1024]{1,0:T(8,128)S(1)}, f32[32,1024]{1,0:T(8,128)}, u32[]{:S(2)}) copy-start(f32[32,1024]{1,0:T(8,128)} %residual.1) | copy-start | bytes 393220
  86.7 7.2 %copy-start.5 = (f32[32,1024]{1,0:T(8,128)S(1)}, f32[32,1024]{1,0:T(8,128)}, u32[]{:S(2)}) copy-start(f32[32,1024]{1,0:T(8,128)} %get-tuple-element.9) | copy-start | bytes 393220
  94.3 1.1 %copy-start.1 = (f32[32,1024]{1,0:T(8,128)}, f32[32,1024]{1,0:T(8,128)S(1)}, u32[]{:S(2)}) copy-start(f32[32,1024]{1,0:T(8,128)S(1)} %convolution_subtract_fusion) | copy-start | bytes 393220
  94.6 0.9 copy-start
  95.5 1.0 %copy-start.4 = (f32[32,1024]{1,0:T(8,128)S(1)}, f32[32,1024]{1,0:T(8,128)}, u32[]{:S(2)}) copy-start(f32[32,1024]{1,0:T(8,128)} %param.11) | copy-start | bytes 393220

commit v3 on v2

--- a/solution.py
+++ b/solution.py
@@ -28,14 +28,55 @@
 
 
 def apply_left(matrix, vectors):
-    return jnp.dot(matrix.T, vectors, precision=HIGHEST)
-
-
-def symmetric_solve(matrix, target):
-    balanced = 0.5 * (matrix + matrix.T)
-    factor = jnp.linalg.cholesky(balanced)
-    middle = lax.linalg.triangular_solve(factor, target, left_side=True, lower=True)
-    return lax.linalg.triangular_solve(factor, middle, left_side=True, lower=True, transpose_a=True)
+    return lax.dot_general(
+        matrix, vectors, (((0,), (0,)), ((), ())), precision=HIGHEST, preferred_element_type=F32
+    )
+
+
+def eliminate(systems):
+    size = systems[0].shape[0]
+    row = lax.broadcasted_iota(jnp.int32, systems[0].shape, 0)
+    for k in range(size):
+        result = []
+        for system in systems:
+            column = jnp.broadcast_to(system[:, k : k + 1], system.shape)
+            scaled = system[k : k + 1] / column[k : k + 1]
+            result.append(jnp.where(row == k, scaled, system - column * scaled))
+        systems = result
+    return systems
+
+
+def update_kernel(
+    gram, applied, solution_field, residual, direction, solution_next, residual_next, direction_next
+):
+    probes = direction.shape[0]
+    sums = gram[...]
+    turned = sums.T
+
+    def part(array, row, col):
+        return array[row * probes : (row + 1) * probes, col * probes : (col + 1) * probes]
+
+    square, image_resid, norm_old = part(sums, 0, 0), part(sums, 0, 1), part(sums, 1, 1)
+    curvature = 0.5 * (part(sums, 0, 2) + part(turned, 2, 0))
+    balanced = 0.5 * (norm_old + part(turned, 1, 1))
+    eye = [lax.broadcasted_iota(jnp.int32, (probes, probes), axis) for axis in (0, 1)]
+    eye = jnp.where(eye[0] == eye[1], 1.0, 0.0)
+    fill = jnp.zeros((probes, TILE - 2 * probes), F32)
+    first, second = eliminate(
+        [
+            jnp.concatenate([curvature, part(turned, 2, 1), fill], axis=1),
+            jnp.concatenate([balanced, eye, fill], axis=1),
+        ]
+    )
+    step_size, inverse = first[:, probes : 2 * probes], second[:, probes : 2 * probes]
+    along = direction[...]
+    solution_next[...] = solution_field[...] + apply_left(step_size, along)
+    remain = residual[...] - apply_left(step_size, applied[...])
+    residual_next[...] = remain
+    mixed = jnp.dot(square, step_size, precision=HIGHEST) - image_resid
+    norm_new = norm_old + apply_left(step_size, mixed) - apply_left(image_resid, step_size)
+    mix_weight = jnp.dot(inverse, norm_new, precision=HIGHEST)
+    direction_next[...] = remain + apply_left(mix_weight, along)
 
 
 @functools.lru_cache(None)
@@ -526,21 +567,13 @@
         compiler_params=pltpu.CompilerParams(collective_id=0, has_side_effects=True),
         name="step",
     )(direction, residual, positions, tile_pairs, pair_count)
-    square, image_resid = gram[:probes, :probes], gram[:probes, probes : 2 * probes]
-    norm_old = gram[probes:, probes : 2 * probes]
-    curvature = gram[:probes, 2 * probes : 3 * probes].T
-    crossing = gram[probes:, 2 * probes : 3 * probes].T
-    step_size = symmetric_solve(curvature, crossing)
-    residual_next = residual - apply_left(step_size, applied)
-    shifted = jnp.dot(step_size.T, image_resid, precision=HIGHEST)
-    quadratic = jnp.dot(
-        step_size.T, jnp.dot(square, step_size, precision=HIGHEST), precision=HIGHEST
-    )
-    norm_new = norm_old - shifted - shifted.T + quadratic
-    solution_next = solution_field + apply_left(step_size, direction)
-    mix_weight = symmetric_solve(norm_old, norm_new)
-    direction_next = residual_next + apply_left(mix_weight, direction)
-    return (solution_next, residual_next, direction_next)
+    return pl.pallas_call(
+        update_kernel,
+        out_shape=(jax.ShapeDtypeStruct((probes, points), F32),) * 3,
+        in_specs=[vmem] * 5,
+        out_specs=(vmem,) * 3,
+        name="update",
+    )(gram, applied, solution_field, residual, direction)
 
 
 def solution(mesh):

time: 97.7 us -> 85.2 us (0.87)
  other arithmetic: 13.5 us -> 0 us
  Pallas kernels: 77.4 us -> 83.8 us
  matrix products: 3.59 us -> 0 us
  local copies, waits for them, and re-layouts: 1.54 us -> 0 us
    another operation x10 -> x0, other arithmetic: 13.4 us -> none  [the longest x6 7.2 us: symmetric_solve(): factor = jnp.linalg.cholesky(balanced)]
    pallas_call x0 -> x1, Pallas kernels: none -> 6.35 us  [on_device(): pl.pallas_call(update_kernel, out_shape=(jax.ShapeDtypeStruct((probes, po...]
    dot_general x6 -> x0, matrix products: 2.86 us -> none  [the longest x3 2.26 us: apply_left(): return jnp.dot(matrix.T, vectors, precision=HIGHEST)]
where the time goes in v3:
time: 85.2 us; the launch traced here: 85.1 us
  Pallas kernels  83.8 us (98%)
  between operations  1.29 us (2%)
    pallas_call x1, Pallas kernels, on_device(): pl.pallas_call(functools.partial(step_kernel, n_row, n_col), out_shape=(j...  77.4 us
    pallas_call x1, Pallas kernels, on_device(): pl.pallas_call(update_kernel, out_shape=(jax.ShapeDtypeStruct((probes, po...  6.35 us

profile of v3, /device:TPU:0, one launch (start us, length us, event | category | flops | bytes accessed | tf_op | source)
XLA Modules:
  0.0 85.1 jit_solution(4269423882766262598)
XLA Ops:
  1.3 77.4 %step.1 = (f32[32,1024]{1,0:T(8,128)}, f32[64,128]{1,0:T(8,128)}) custom-call(f32[32,1024]{1,0:T(8,128)} %direction.3, f32[32,1024]{1,0:T(8,128)} %residual.3, bf16[2,1024]{1,0:T(2,128)(2,1)} %positions.1, s32[2,1536]{1,0:T(2,128)} %tile_pairs.1, s32[1]{0:T(128)S(6)} %copy.9.count), custom_call_target="tpu_custom_call" | custom-call | tf_op jit(solution)/shard_map/step/pallas_call | solution.py:538
  78.7 6.4 %update.1 = (f32[32,1024]{1,0:T(8,128)}, f32[32,1024]{1,0:T(8,128)}, f32[32,1024]{1,0:T(8,128)}) custom-call(f32[64,128]{1,0:T(8,128)} %get-tuple-element.5.gram, f32[32,1024]{1,0:T(8,128)} %get-tuple-element.6.applied, f32[32,1024]{1,0:T(8,128)} %solution_field.1, f32[32,1024]{1,0:T(8,128)} %residual.3, f32[32,1024]{1,0:T(8,128)} %direction.3), custom_call_target="tpu_custom_call" | custom-call | tf_op jit(solution)/shard_map/update/pallas_call | solution.py:570

commit v4 on v3

--- a/solution.py
+++ b/solution.py
@@ -179,14 +179,18 @@
         return place[0] * self.n_col + place[1]
 
     def greet(self):
-        barrier = pltpu.get_barrier_semaphore()
         offsets = [(r, c) for r in range(self.n_row) for c in range(self.n_col)][1:]
         for offset in offsets:
             row, col = self.plus(offset)
             pl.semaphore_signal(
-                barrier, inc=1, device_id={"row": row, "col": col}, device_id_type=MESH
+                pltpu.get_barrier_semaphore(),
+                inc=1,
+                device_id={"row": row, "col": col},
+                device_id_type=MESH,
             )
-        pl.semaphore_wait(barrier, len(offsets))
+
+    def wait_greeted(self):
+        pl.semaphore_wait(pltpu.get_barrier_semaphore(), self.n_row * self.n_col - 1)
 
 
 def remote(source, landing, send_sem, recv_sem, place):
@@ -231,8 +235,8 @@
 
 
 def kernel_of(differ_x, differ_y):
-    square = (differ_x * differ_x + differ_y * differ_y).astype(F32)
-    square = jnp.minimum(jnp.maximum(square, 1e-20), SCALE * SCALE)
+    square = differ_x * differ_x + differ_y * differ_y
+    square = jnp.minimum(jnp.maximum(square, BF16(1e-20)), BF16(SCALE * SCALE)).astype(F32)
     quad = square * lax.rsqrt(square)
     remain = SCALE - quad
     remain = remain * remain
@@ -284,12 +288,14 @@
 
 def batches_of(n_row, n_col):
     cover, units = cover_of(n_row, n_col), list(units_of(n_row, n_col))
+    start = len(cover) // 2
+    order = [start] + [s for s in range(len(cover) - 1, 0, -1) if s != start]
     result, waited = [], {0}
-    for slot in range(1, len(cover)):
+    for slot in order:
         mine = sorted((u for u in units if slot in u), key=lambda u: (sum(u) - slot, u))
         units = [u for u in units if slot not in u]
-        cut = [u for u in mine if sum(u) - slot <= len(cover) // 2]
-        pieces = [cut, mine[len(cut) :]] if slot == 1 else [mine]
+        cut = [u for u in mine if sum(u) - slot < start]
+        pieces = [cut, mine[len(cut) :]] if slot == start else [mine]
         pieces = [piece for piece in pieces if piece]
         for k, piece in enumerate(pieces):
             need = sorted({s for u in piece for s in u} - waited)
@@ -334,11 +340,12 @@
     scale = AMPLITUDE / 256.0
     me = ring.flat((ring.row, ring.col))
 
+    ring.greet()
     dirs[0] = direction[...].astype(BF16)
     places[0] = positions[...]
     table, own_table = pattern(ring, tiles, group, tile_pairs, count[0])
     tables[me] = table.reshape(tables.shape[1:]).astype(BF16)
-    ring.greet()
+    ring.wait_greeted()
     sends = []
     for s, offset in enumerate(cover[1:], 1):
         place = ring.minus(offset)
@@ -417,7 +424,7 @@
 
     rows_of, cols_of = [o[0] for o in cover], [o[1] for o in cover]
 
-    def unit(i, j):
+    def prepare(i, j):
         row_i, col_i = ring.plus((pick(i, rows_of), pick(i, cols_of)))
         row_j, col_j = ring.plus((pick(j, rows_of), pick(j, cols_of)))
         swap = (row_i * n_col + col_i - row_j * n_col - col_j + n_row * n_col) // (n_row * n_col)
@@ -431,7 +438,9 @@
         start = (col_low % group) * (n_row * tiles) + row_high * tiles
         mask = pltpu.roll(table, lax.rem(lanes - start, lanes), 1)
         set_far(high, mask[:, :TILE], places, widen, far_x, far_y)
-        first = swap * half
+        return low, high, swap * half
+
+    def unit(low, high, first):
         forward = [None] * half
         backward = [None] * blocks
         for a in range(half):
@@ -449,14 +458,22 @@
         for b in range(blocks):
             acc[high, :, b * BLOCK : (b + 1) * BLOCK] += backward[b]
 
-    for k, (need, units, complete) in enumerate(batches_of(n_row, n_col)):
+    batches = batches_of(n_row, n_col)
+    every = [u for _, units, _ in batches for u in units]
+    state = prepare(jnp.int32(every[0][0]), jnp.int32(every[0][1]))
+    done = 0
+    for k, (need, units, complete) in enumerate(batches):
         for s in need:
             origin = ring.plus(cover[s])
             remote(dirs.at[0], dirs.at[s], sems[4].at[s], sems[5].at[s], origin).wait_recv()
-
-        @pl.loop(0, len(units))
-        def _(t):
-            unit(pick(t, [u[0] for u in units]), pick(t, [u[1] for u in units]))
+        done += len(units)
+        coming = units[1:] + [every[done % len(every)]]
+
+        def one(t, now):
+            unit(*now)
+            return prepare(pick(t, [u[0] for u in coming]), pick(t, [u[1] for u in coming]))
+
+        state = lax.fori_loop(0, len(units), one, state)
 
         if k == 0:
             early_col.wait_recv()

time: 85.2 us -> 76 us (0.89)
  Pallas kernels: 83.8 us -> 74.5 us
    pallas_call x1, Pallas kernels: 77.4 us -> 68.2 us  [on_device(): pl.pallas_call(functools.partial(step_kernel, n_row, n_col), out_shape=(j...]
where the time goes in v4:
time: 76 us; the launch traced here: 75.8 us
  Pallas kernels  74.5 us (98%)
  between operations  1.29 us (2%)
    pallas_call x1, Pallas kernels, on_device(): pl.pallas_call(functools.partial(step_kernel, n_row, n_col), out_shape=(j...  68.2 us
    pallas_call x1, Pallas kernels, on_device(): pl.pallas_call(update_kernel, out_shape=(jax.ShapeDtypeStruct((probes, po...  6.36 us

profile of v4, /device:TPU:0, one launch (start us, length us, event | category | flops | bytes accessed | tf_op | source)
XLA Modules:
  0.0 75.8 jit_solution(2215185585791421100)
XLA Ops:
  1.3 68.2 %step.1 = (f32[32,1024]{1,0:T(8,128)}, f32[64,128]{1,0:T(8,128)}) custom-call(f32[32,1024]{1,0:T(8,128)} %direction.3, f32[32,1024]{1,0:T(8,128)} %residual.3, bf16[2,1024]{1,0:T(2,128)(2,1)} %positions.1, s32[2,1536]{1,0:T(2,128)} %tile_pairs.1, s32[1]{0:T(128)S(6)} %copy.9.count), custom_call_target="tpu_custom_call" | custom-call | tf_op jit(solution)/shard_map/step/pallas_call | solution.py:555
  69.5 6.4 %update.1 = (f32[32,1024]{1,0:T(8,128)}, f32[32,1024]{1,0:T(8,128)}, f32[32,1024]{1,0:T(8,128)}) custom-call(f32[64,128]{1,0:T(8,128)} %get-tuple-element.5.gram, f32[32,1024]{1,0:T(8,128)} %get-tuple-element.6.applied, f32[32,1024]{1,0:T(8,128)} %solution_field.1, f32[32,1024]{1,0:T(8,128)} %residual.3, f32[32,1024]{1,0:T(8,128)} %direction.3), custom_call_target="tpu_custom_call" | custom-call | tf_op jit(solution)/shard_map/update/pallas_call | solution.py:587

commit v5 on v4

--- a/solution.py
+++ b/solution.py
@@ -294,13 +294,34 @@
     for slot in order:
         mine = sorted((u for u in units if slot in u), key=lambda u: (sum(u) - slot, u))
         units = [u for u in units if slot not in u]
-        cut = [u for u in mine if sum(u) - slot < start]
-        pieces = [cut, mine[len(cut) :]] if slot == start else [mine]
-        pieces = [piece for piece in pieces if piece]
+        pieces = [mine]
+        if slot == start:
+            others = sorted({sum(u) - slot for u in mine})
+            rest = len(others) - 1
+            cuts = [0, 1] + [1 + k * rest // 3 for k in (1, 2, 3)]
+            pieces = [
+                [u for u in mine if sum(u) - slot in others[a:b]] for a, b in zip(cuts, cuts[1:])
+            ]
+            pieces = [piece for piece in pieces if piece]
         for k, piece in enumerate(pieces):
             need = sorted({s for u in piece for s in u} - waited)
             waited |= set(need)
             result.append((need, piece, slot if k == len(pieces) - 1 else None))
+    return result
+
+
+def tables_of(n_row, n_col):
+    cover, batches = cover_of(n_row, n_col), batches_of(n_row, n_col)
+    every = [u for _, units, _ in batches for u in units]
+    result, seen, done = [], {(0, 0)}, 0
+    for count in [1] + [len(units) for _, units, _ in batches]:
+        reach = every[: done + 1] if not result else every[: done + count + 1]
+        done += count if result else 0
+        used = [o for i, j in reach for o in ((i, j), (j, i))]
+        used = [(cover[i][0], cover[j][1]) for i, j in used]
+        new = [o for o in dict.fromkeys(used) if o not in seen]
+        seen |= set(new)
+        result.append(new)
     return result
 
 
@@ -346,16 +367,29 @@
     table, own_table = pattern(ring, tiles, group, tile_pairs, count[0])
     tables[me] = table.reshape(tables.shape[1:]).astype(BF16)
     ring.wait_greeted()
+    batches, wanted = batches_of(n_row, n_col), tables_of(n_row, n_col)
     sends = []
     for s, offset in enumerate(cover[1:], 1):
         place = ring.minus(offset)
         sends.append(remote(places.at[0], places.at[s], sems[2].at[s], sems[3].at[s], place))
-    for k, offset in enumerate(holders):
-        place = ring.minus(offset)
-        sends.append(remote(tables.at[me], tables.at[me], sems[0].at[k], sems[1].at[k], place))
-    for s, offset in enumerate(cover[1:], 1):
-        place = ring.minus(offset)
-        sends.append(remote(dirs.at[0], dirs.at[s], sems[4].at[s], sems[5].at[s], place))
+
+    def send_tables(offsets):
+        for offset in offsets:
+            k, at = holders.index(offset), tables.at[me]
+            sends.append(remote(at, at, sems[0].at[k], sems[1].at[k], ring.minus(offset)))
+
+    def wait_tables(offsets):
+        for offset in offsets:
+            k, origin = holders.index(offset), ring.plus(offset)
+            at = tables.at[ring.flat(origin)]
+            remote(at, at, sems[0].at[k], sems[1].at[k], origin).wait_recv()
+
+    send_tables(wanted[0])
+    for (need, _, _), offsets in zip(batches, wanted[1:]):
+        for s in need:
+            place = ring.minus(cover[s])
+            sends.append(remote(dirs.at[0], dirs.at[s], sems[4].at[s], sems[5].at[s], place))
+        send_tables(offsets)
     for copy in sends:
         copy.start()
 
@@ -417,11 +451,7 @@
     def _(slot):
         spread_places(slot, places, near_x, near_y)
 
-    for k, offset in enumerate(holders):
-        origin = ring.plus(offset)
-        at = tables.at[ring.flat(origin)]
-        remote(at, at, sems[0].at[k], sems[1].at[k], origin).wait_recv()
-
+    wait_tables(wanted[0])
     rows_of, cols_of = [o[0] for o in cover], [o[1] for o in cover]
 
     def prepare(i, j):
@@ -458,7 +488,6 @@
         for b in range(blocks):
             acc[high, :, b * BLOCK : (b + 1) * BLOCK] += backward[b]
 
-    batches = batches_of(n_row, n_col)
     every = [u for _, units, _ in batches for u in units]
     state = prepare(jnp.int32(every[0][0]), jnp.int32(every[0][1]))
     done = 0
@@ -466,6 +495,7 @@
         for s in need:
             origin = ring.plus(cover[s])
             remote(dirs.at[0], dirs.at[s], sems[4].at[s], sems[5].at[s], origin).wait_recv()
+        wait_tables(wanted[k + 1])
         done += len(units)
         coming = units[1:] + [every[done % len(every)]]
 
@@ -475,11 +505,11 @@
 
         state = lax.fori_loop(0, len(units), one, state)
 
-        if k == 0:
+        if k == len(batches) // 3:
             early_col.wait_recv()
             sum_cols(1)
             early_row.start()
-        if k == 1:
+        if k == 2 * len(batches) // 3:
             early_row.wait_recv()
             sum_rows(1)
         if complete is not None:

time: 76 us -> 72.8 us (0.958)
  Pallas kernels: 74.5 us -> 71.4 us
    pallas_call x1, Pallas kernels: 68.2 us -> 65 us  [on_device(): pl.pallas_call(functools.partial(step_kernel, n_row, n_col), out_shape=(j...]
where the time goes in v5:
time: 72.8 us; the launch traced here: 72.7 us
  Pallas kernels  71.4 us (98%)
  between operations  1.29 us (2%)
    pallas_call x1, Pallas kernels, on_device(): pl.pallas_call(functools.partial(step_kernel, n_row, n_col), out_shape=(j...  65 us
    pallas_call x1, Pallas kernels, on_device(): pl.pallas_call(update_kernel, out_shape=(jax.ShapeDtypeStruct((probes, po...  6.35 us

profile of v5, /device:TPU:0, one launch (start us, length us, event | category | flops | bytes accessed | tf_op | source)
XLA Modules:
  0.0 72.7 jit_solution(12579088006877286331)
XLA Ops:
  1.3 65.0 %step.1 = (f32[32,1024]{1,0:T(8,128)}, f32[64,128]{1,0:T(8,128)}) custom-call(f32[32,1024]{1,0:T(8,128)} %direction.3, f32[32,1024]{1,0:T(8,128)} %residual.3, bf16[2,1024]{1,0:T(2,128)(2,1)} %positions.1, s32[2,1536]{1,0:T(2,128)} %tile_pairs.1, s32[1]{0:T(128)S(6)} %copy.9.count), custom_call_target="tpu_custom_call" | custom-call | tf_op jit(solution)/shard_map/step/pallas_call | solution.py:585
  66.3 6.3 %update.1 = (f32[32,1024]{1,0:T(8,128)}, f32[32,1024]{1,0:T(8,128)}, f32[32,1024]{1,0:T(8,128)}) custom-call(f32[64,128]{1,0:T(8,128)} %get-tuple-element.5.gram, f32[32,1024]{1,0:T(8,128)} %get-tuple-element.6.applied, f32[32,1024]{1,0:T(8,128)} %solution_field.1, f32[32,1024]{1,0:T(8,128)} %residual.3, f32[32,1024]{1,0:T(8,128)} %direction.3), custom_call_target="tpu_custom_call" | custom-call | tf_op jit(solution)/shard_map/update/pallas_call | solution.py:617
